TPU v7x, 256 devices: a whole 4x4x8 slice. The times are simulated.
256 devices in a mesh: dp: 4 (over y), expert: 64 (over x, z, core).
Axes of the slice: x: 4, y: 4, z: 8, core: 2. Of those that a mesh axis runs over, the one named last changes fastest.
Arguments:
- tokens: bfloat16 [8192, 2048], P(('dp', 'expert')), may hold values from -6 to 6
- grad_out: bfloat16 [8192, 2048], P(('dp', 'expert')), may hold values from -0.59765625 to 0.59765625
- routing: int32 [8192, 8], P(('dp', 'expert')), may hold values from 0 to 127, as said below
- replica: int32 [8192, 8], P(('dp', 'expert')), may hold values from 0 to 1, as said below
- gates: bfloat16 [8192, 8], P(('dp', 'expert')), may hold values from 0.25 to 4
- host_expert: int32 [64], replicated, may hold values from 0 to 127, as said below
- w_gate_up: bfloat16 [128, 2, 768, 2048], P('expert', None, 'dp'), may hold values from -0.125 to 0.125
- w_down: bfloat16 [128, 768, 2048], P('expert', 'dp'), may hold values from -0.21875 to 0.21875
Outputs:
- grad_tokens: bfloat16 [8192, 2048], P(('dp', 'expert'))
- grad_gates: float32 [8192, 8], P(('dp', 'expert'))
- grad_w_gate_up: bfloat16 [128, 2, 768, 2048], P('expert', None, 'dp')
- grad_w_down: bfloat16 [128, 768, 2048], P('expert', 'dp')
Inputs may be any that keep to these rules, and one draw needn't show every extreme that they name: `routing`: column k of a token names an expert of 16 * k to 16 * k + 15. Within the rows of one device, experts 2 i and 2 i + 1 are named together exactly 2 * 2 times. `replica`: within the rows of one device, each expert has at most 2 choices marked 0 and at most 2 marked 1; some expert reaches 2 marked 0 from every device, and in every index of dp some expert reaches 2 marked 1 from every device. Only experts listed in host_expert have choices marked 1. `host_expert`: for every device d of the expert axis exactly one of its experts 2 d and 2 d + 1 is listed, and it is listed once.
All inputs are finite; a program needn't handle non-finite values.
Results may differ from a plain program's by a relative error of at most 0.013.
Values may be sent and summed in bfloat16 or wider, within the bound.
No kernel may reach another device: no remote copies, remote signals or barrier semaphores. Data moves between devices by JAX's collectives and lax.ppermute only.
A program may use at most 128 MiB of HBM per device.

v0:
```python
import math

import jax
import jax.numpy as jnp
from jax import lax
from jax.sharding import PartitionSpec as P


def in_one_piece(arrays, axis, split_dim, concat_dim, along):
    columns = [a.reshape(*a.shape[:along], -1) for a in arrays]
    both = jnp.concatenate(columns, axis=along)
    whole, at, gathered = (
        lax.all_to_all(both, axis, split_axis=split_dim, concat_axis=concat_dim, tiled=True),
        0,
        [],
    )
    for a, column in zip(arrays, columns):
        slab = whole[..., at : at + column.shape[along]]
        gathered.append(slab.reshape(*slab.shape[:along], *a.shape[along:]))
        at += column.shape[along]
    return tuple(gathered)


def in_one_piece_2(arrays, axis, dim, along):
    widths = [math.prod(a.shape[along:]) for a in arrays]
    both = jnp.concatenate(
        [a.reshape(*a.shape[:along], w) for a, w in zip(arrays, widths)], axis=along
    )
    whole = lax.all_gather(both, axis, axis=dim, tiled=True)
    pieces = jnp.split(whole, [sum(widths[:k]) for k in range(1, len(widths))], axis=along)
    return tuple(
        (b.reshape(*whole.shape[:along], *a.shape[along:]) for a, b in zip(arrays, pieces))
    )


def sent_together(arrays, axis, dim, along):
    widths = [math.prod(a.shape[along:]) for a in arrays]
    both = jnp.concatenate(
        [a.reshape(*a.shape[:along], w) for a, w in zip(arrays, widths)], axis=along
    )
    whole = lax.psum_scatter(both, axis, scatter_dimension=dim, tiled=True)
    pieces = jnp.split(whole, [sum(widths[:k]) for k in range(1, len(widths))], axis=along)
    return tuple(
        (b.reshape(*whole.shape[:along], *a.shape[along:]) for a, b in zip(arrays, pieces))
    )


def lookup(values_table, indices):
    matches = indices[..., None] == lax.broadcasted_iota(
        jnp.int32, indices.shape + values_table.shape, indices.ndim
    )
    return jnp.sum(jnp.where(matches, values_table, 0), axis=-1)


def placement(host_expert, owned_experts, devices):
    experts = owned_experts * devices
    matches = host_expert[None, :] == lax.broadcasted_iota(jnp.int32, (experts, devices), 0)
    helper_ids = lax.broadcasted_iota(jnp.int32, (experts, devices), 1)
    helper_of = jnp.sum(jnp.where(matches, helper_ids, 0), axis=1)
    listed = jnp.sum(matches.astype(jnp.int32), axis=1)
    return (helper_of, listed)


def targets(routing, replica, host_expert, owned_experts, devices, slot_rows, groups):
    helper_of, listed = placement(host_expert, owned_experts, devices)
    choices = routing.shape[0] // groups * routing.shape[1]
    usable = (replica == 0) | (lookup(listed, routing) > 0)
    device_to = jnp.where(replica == 0, routing // owned_experts, lookup(helper_of, routing))
    block_to = jnp.where(replica == 0, routing % owned_experts, owned_experts)
    labels = (routing * 2 + replica).reshape(groups, choices)
    earlier = lax.broadcasted_iota(jnp.int32, (choices, choices), 1) < lax.broadcasted_iota(
        jnp.int32, (choices, choices), 0
    )
    matching = (labels[:, :, None] == labels[:, None, :]) & earlier[None]
    ranking = jnp.sum(matching.astype(jnp.int32), axis=2).reshape(routing.shape)
    group_ids = lax.broadcasted_iota(jnp.int32, (groups, choices), 0).reshape(routing.shape)
    position = ((block_to * groups + group_ids) * devices + device_to) * slot_rows + ranking
    return jnp.where(usable, position, -1)


def selector(position, total_slots):
    matches = position[None, :, :] == lax.broadcasted_iota(
        jnp.int32, (total_slots,) + position.shape, 0
    )
    picker = jnp.sum(matches.astype(jnp.float32), axis=2).astype(jnp.bfloat16)
    return (matches, picker)


def fill_rows(matches, picker, tokens, grad_out, gates):
    row_x = jnp.dot(picker, tokens, preferred_element_type=jnp.float32).astype(jnp.bfloat16)
    row_dy = jnp.dot(picker, grad_out, preferred_element_type=jnp.float32).astype(jnp.bfloat16)
    row_gate = jnp.sum(
        jnp.where(matches, gates[None].astype(jnp.float32), 0.0), axis=(1, 2)
    ).astype(jnp.bfloat16)
    return (row_x, row_dy, row_gate)


def expert_block(inputs, upstream, weight, gate_up, down_matrix):
    mixed = jnp.einsum("rd,jfd->jrf", inputs, gate_up, preferred_element_type=jnp.float32)
    gate_pre = mixed[0]
    up_part = mixed[1]
    sigmoid_gate = jax.nn.sigmoid(gate_pre)
    active = gate_pre * sigmoid_gate
    hidden = (active * up_part).astype(jnp.bfloat16)
    output_part = jnp.einsum("rf,fd->rd", hidden, down_matrix, preferred_element_type=jnp.float32)
    gate_part = jnp.sum(output_part * upstream.astype(jnp.float32), axis=1)
    scaled = (weight.astype(jnp.float32)[:, None] * upstream.astype(jnp.float32)).astype(
        jnp.bfloat16
    )
    grad_hidden = jnp.einsum("rd,fd->rf", scaled, down_matrix, preferred_element_type=jnp.float32)
    grad_gate = grad_hidden * up_part * sigmoid_gate * (1.0 + gate_pre * (1.0 - sigmoid_gate))
    grad_mixed = jnp.stack([grad_gate, grad_hidden * active], axis=0).astype(jnp.bfloat16)
    input_part = jnp.einsum("jrf,jfd->rd", grad_mixed, gate_up, preferred_element_type=jnp.float32)
    weight_gu = jnp.einsum("jrf,rd->jfd", grad_mixed, inputs, preferred_element_type=jnp.float32)
    weight_down = jnp.einsum("rf,rd->fd", hidden, scaled, preferred_element_type=jnp.float32)
    return (input_part, gate_part, weight_gu, weight_down)


def shards(tokens, grad_out, routing, replica, gates, host_expert, w_gate_up, w_down):
    devices = lax.axis_size("expert")
    device_id = lax.axis_index("expert")
    token_rows, features = tokens.shape
    owned_experts = w_gate_up.shape[0]
    quarter = w_down.shape[1]
    topk_width = routing.shape[1]
    slot_rows = token_rows * topk_width // (owned_experts * devices)
    blocks = owned_experts + 1
    lane_rows = devices * slot_rows
    piece_rows = quarter // devices
    home_slots = targets(routing, replica, host_expert, owned_experts, devices, slot_rows, 1)
    home_matches, home_picker = selector(home_slots, blocks * lane_rows)
    row_x, row_dy, row_gate = fill_rows(home_matches, home_picker, tokens, grad_out, gates)
    sent_x, sent_dy, sent_gate = in_one_piece(
        (
            row_x.reshape(blocks, lane_rows, features),
            row_dy.reshape(blocks, lane_rows, features),
            row_gate.reshape(blocks, lane_rows),
        ),
        "expert",
        1,
        1,
        2,
    )
    block_x, block_dy, block_gate = in_one_piece_2((sent_x, sent_dy, sent_gate), "dp", 1, 2)
    owner_of_helper = host_expert // owned_experts
    owns_copy = owner_of_helper == device_id
    copied_local = jnp.sum(jnp.where(owns_copy, host_expert % owned_experts, 0))
    helper_ids = lax.broadcasted_iota(jnp.int32, (devices, devices), 1)
    owner_ids = lax.broadcasted_iota(jnp.int32, (devices, devices), 0)
    helper_of_owner = jnp.sum(
        jnp.where(owner_of_helper[None, :] == owner_ids, helper_ids, 0), axis=1
    )
    source_gu = lax.dynamic_index_in_dim(w_gate_up, copied_local, 0, keepdims=False)
    source_down = lax.dynamic_index_in_dim(w_down, copied_local, 0, keepdims=False)
    spread_gu, spread_down = (
        lax.all_to_all(
            source_gu.reshape(2, devices, piece_rows, features),
            "expert",
            split_axis=1,
            concat_axis=1,
            tiled=True,
        ),
        lax.all_to_all(
            source_down.reshape(1, devices, piece_rows, features),
            "expert",
            split_axis=1,
            concat_axis=1,
            tiled=True,
        ),
    )
    spread_gu = jnp.take(spread_gu, owner_of_helper, axis=1)
    spread_down = jnp.take(spread_down, owner_of_helper, axis=1)
    hosted_gu, hosted_down = (
        lax.all_to_all(spread_gu, "expert", split_axis=1, concat_axis=1, tiled=True),
        lax.all_to_all(spread_down, "expert", split_axis=1, concat_axis=1, tiled=True),
    )
    hosted_gu = hosted_gu.reshape(2, quarter, features)
    hosted_down = hosted_down.reshape(quarter, features)
    input_parts = []
    gate_parts = []
    owner_gu = []
    owner_down = []
    for block in range(blocks):
        if block < owned_experts:
            gate_up = w_gate_up[block]
            down_matrix = w_down[block]
        else:
            gate_up = hosted_gu
            down_matrix = hosted_down
        input_part, gate_part, weight_gu, weight_down = expert_block(
            block_x[block], block_dy[block], block_gate[block], gate_up, down_matrix
        )
        input_parts.append(input_part.astype(jnp.bfloat16))
        gate_parts.append(gate_part.astype(jnp.bfloat16))
        owner_gu.append(weight_gu)
        owner_down.append(weight_down)
    helper_gu = owner_gu[owned_experts].astype(jnp.bfloat16)
    helper_down = owner_down[owned_experts].astype(jnp.bfloat16)
    back_gu, back_down = (
        lax.all_to_all(
            helper_gu.reshape(2, devices, piece_rows, features),
            "expert",
            split_axis=1,
            concat_axis=1,
            tiled=True,
        ),
        lax.all_to_all(
            helper_down.reshape(1, devices, piece_rows, features),
            "expert",
            split_axis=1,
            concat_axis=1,
            tiled=True,
        ),
    )
    back_gu = jnp.take(back_gu, helper_of_owner, axis=1)
    back_down = jnp.take(back_down, helper_of_owner, axis=1)
    extra_gu, extra_down = (
        lax.all_to_all(back_gu, "expert", split_axis=1, concat_axis=1, tiled=True),
        lax.all_to_all(back_down, "expert", split_axis=1, concat_axis=1, tiled=True),
    )
    extra_gu = extra_gu.reshape(2, quarter, features).astype(jnp.float32)
    extra_down = extra_down.reshape(quarter, features).astype(jnp.float32)
    stacked_dx = jnp.stack(input_parts, axis=0)
    stacked_dg = jnp.stack(gate_parts, axis=0)
    summed_dx, summed_dg = tuple(
        (part.astype(jnp.float32) for part in sent_together((stacked_dx, stacked_dg), "dp", 1, 2))
    )
    row_dx = summed_dx.astype(jnp.bfloat16)
    row_dg = summed_dg.astype(jnp.bfloat16)
    home_dx, home_dg = (
        lax.all_to_all(row_dx, "expert", split_axis=1, concat_axis=1, tiled=True),
        lax.all_to_all(row_dg, "expert", split_axis=1, concat_axis=1, tiled=True),
    )
    home_dx = home_dx.reshape(blocks * lane_rows, features)
    home_dg = home_dg.reshape(blocks * lane_rows).astype(jnp.float32)
    grad_tokens = jnp.einsum(
        "st,sd->td", home_picker, home_dx, preferred_element_type=jnp.float32
    ).astype(jnp.bfloat16)
    grad_gates = jnp.sum(jnp.where(home_matches, home_dg[:, None, None], 0.0), axis=0)
    grad_gu = []
    grad_down = []
    for block in range(owned_experts):
        present = (copied_local == block).astype(jnp.float32)
        grad_gu.append((owner_gu[block] + present * extra_gu).astype(jnp.bfloat16))
        grad_down.append((owner_down[block] + present * extra_down).astype(jnp.bfloat16))
    return (grad_tokens, grad_gates, jnp.stack(grad_gu, axis=0), jnp.stack(grad_down, axis=0))


def solution(mesh):
    in_specs = (
        P(("dp", "expert"), None),
        P(("dp", "expert"), None),
        P(("dp", "expert"), None),
        P(("dp", "expert"), None),
        P(("dp", "expert"), None),
        P(),
        P("expert", None, "dp", None),
        P("expert", "dp", None),
    )
    out_specs = (
        P(("dp", "expert"), None),
        P(("dp", "expert"), None),
        P("expert", None, "dp", None),
        P("expert", "dp", None),
    )
    return jax.shard_map(shards, mesh=mesh, in_specs=in_specs, out_specs=out_specs, check_vma=False)
```

profile of v0, /device:TPU:1, one launch (start us, length us, event | category | flops | bytes accessed | tf_op | source)
XLA Modules:
  0.0 580.6 jit_solution(17716234020058284879)
XLA Ops:
  21.3 113.0 %all_to_all.59 = bf16[3,128,4097]{2,0,1:T(4,128)(2,1)S(1)} all-to-all(bf16[3,128,4097]{2,0,1:T(4,128)(2,1)S(1)} %pad_maximum_fusion.1), channel_id=1, replica_groups=mesh['dp'=4,'expert'=64] {'expert'}, dimensions={1} | all-to-all | bytes 6292992 | tf_op jit(solution)/shard_map/all_to_all | solution.py:13
  141.0 4.9 all-to-all-start.1
  150.5 23.9 %all-to-all-done.1 = bf16[1,64,3,2048]{3,2,0,1:T(4,128)(2,1)S(1)} async-done(((bf16[1,64,3,2048]{3,2,0,1:T(4,128)(2,1)}), bf16[1,64,3,2048]{3,2,0,1:T(4,128)(2,1)S(1)}, u32[]{:S(2)}, u32[]{:S(2)}) %all-to-all-start.1) | async-done | bytes 786464 | tf_op jit(solution)/shard_map/all_to_all | solution.py:163
  174.4 6.5 %all-to-all-start.3 = ((bf16[2,64,3,2048]{3,0,2,1:T(2,128)(2,1)}), bf16[2,64,3,2048]{3,0,2,1:T(2,128)(2,1)S(1)}, u32[]{:S(2)}, u32[]{:S(2)}) async-start(bf16[2,64,3,2048]{3,0,2,1:T(2,128)(2,1)} %bitcast.32), calls=%async_computation.3 | async-start | bytes 3145728 | tf_op jit(solution)/shard_map/all_to_all | solution.py:156
  185.2 35.4 %all-to-all-done.3 = bf16[2,64,3,2048]{3,0,2,1:T(2,128)(2,1)S(1)} async-done(((bf16[2,64,3,2048]{3,0,2,1:T(2,128)(2,1)}), bf16[2,64,3,2048]{3,0,2,1:T(2,128)(2,1)S(1)}, u32[]{:S(2)}, u32[]{:S(2)}) %all-to-all-start.3) | async-done | bytes 1572896 | tf_op jit(solution)/shard_map/all_to_all | solution.py:156
  220.6 6.3 %all-to-all-start.2 = ((bf16[1,64,3,2048]{3,2,0,1:T(4,128)(2,1)}), bf16[1,64,3,2048]{3,2,0,1:T(4,128)(2,1)}, u32[]{:S(2)}, u32[]{:S(2)}) async-start(bf16[1,64,3,2048]{3,2,0,1:T(4,128)(2,1)} %fusion.48), calls=%async_computation.2 | async-start | bytes 2097152 | tf_op jit(solution)/shard_map/all_to_all | solution.py:175
  233.3 22.1 %all-to-all-done.2 = bf16[1,64,3,2048]{3,2,0,1:T(4,128)(2,1)} async-done(((bf16[1,64,3,2048]{3,2,0,1:T(4,128)(2,1)}), bf16[1,64,3,2048]{3,2,0,1:T(4,128)(2,1)}, u32[]{:S(2)}, u32[]{:S(2)}) %all-to-all-start.2) | async-done | bytes 786464 | tf_op jit(solution)/shard_map/all_to_all | solution.py:175
  255.4 6.2 %all-to-all-start.4 = ((bf16[2,64,3,2048]{3,0,2,1:T(2,128)(2,1)}), bf16[2,64,3,2048]{3,0,2,1:T(2,128)(2,1)S(1)}, u32[]{:S(2)}, u32[]{:S(2)}) async-start(bf16[2,64,3,2048]{3,0,2,1:T(2,128)(2,1)} %fusion.30), calls=%async_computation.4 | async-start | bytes 3145728 | tf_op jit(solution)/shard_map/all_to_all | solution.py:174
  264.5 36.9 %all-to-all-done.4 = bf16[2,64,3,2048]{3,0,2,1:T(2,128)(2,1)S(1)} async-done(((bf16[2,64,3,2048]{3,0,2,1:T(2,128)(2,1)}), bf16[2,64,3,2048]{3,0,2,1:T(2,128)(2,1)S(1)}, u32[]{:S(2)}, u32[]{:S(2)}) %all-to-all-start.4) | async-done | bytes 1572896 | tf_op jit(solution)/shard_map/all_to_all | solution.py:174
  304.6 4.1 fusion.44
  337.5 6.1 %all-to-all-start.9 = ((bf16[1,64,3,2048]{3,2,0,1:T(4,128)(2,1)}), bf16[1,64,3,2048]{3,2,0,1:T(4,128)(2,1)S(1)}, u32[]{:S(2)}, u32[]{:S(2)}) async-start(bf16[1,64,3,2048]{3,2,0,1:T(4,128)(2,1)} %bitcast.59), calls=%async_computation.10 | async-start | bytes 2097152 | tf_op jit(solution)/shard_map/all_to_all | solution.py:207
  349.0 23.2 %all-to-all-done.9 = bf16[1,64,3,2048]{3,2,0,1:T(4,128)(2,1)S(1)} async-done(((bf16[1,64,3,2048]{3,2,0,1:T(4,128)(2,1)}), bf16[1,64,3,2048]{3,2,0,1:T(4,128)(2,1)S(1)}, u32[]{:S(2)}, u32[]{:S(2)}) %all-to-all-start.9) | async-done | bytes 786464 | tf_op jit(solution)/shard_map/all_to_all | solution.py:207
  372.2 6.2 %all-to-all-start.7 = ((bf16[2,64,3,2048]{3,0,2,1:T(2,128)(2,1)}), bf16[2,64,3,2048]{3,0,2,1:T(2,128)(2,1)S(1)}, u32[]{:S(2)}, u32[]{:S(2)}) async-start(bf16[2,64,3,2048]{3,0,2,1:T(2,128)(2,1)} %bitcast.53), calls=%async_computation.8 | async-start | bytes 3145728 | tf_op jit(solution)/shard_map/all_to_all | solution.py:200
  382.8 35.4 %all-to-all-done.7 = bf16[2,64,3,2048]{3,0,2,1:T(2,128)(2,1)S(1)} async-done(((bf16[2,64,3,2048]{3,0,2,1:T(2,128)(2,1)}), bf16[2,64,3,2048]{3,0,2,1:T(2,128)(2,1)S(1)}, u32[]{:S(2)}, u32[]{:S(2)}) %all-to-all-start.7) | async-done | bytes 1572896 | tf_op jit(solution)/shard_map/all_to_all | solution.py:200
  418.2 6.7 %all-to-all-start.10 = ((bf16[1,64,3,2048]{3,2,0,1:T(4,128)(2,1)}), bf16[1,64,3,2048]{3,2,0,1:T(4,128)(2,1)}, u32[]{:S(2)}, u32[]{:S(2)}) async-start(bf16[1,64,3,2048]{3,2,0,1:T(4,128)(2,1)} %fusion.47), calls=%async_computation.11 | async-start | bytes 2097152 | tf_op jit(solution)/shard_map/all_to_all | solution.py:219
  431.3 21.9 %all-to-all-done.10 = bf16[1,64,3,2048]{3,2,0,1:T(4,128)(2,1)} async-done(((bf16[1,64,3,2048]{3,2,0,1:T(4,128)(2,1)}), bf16[1,64,3,2048]{3,2,0,1:T(4,128)(2,1)}, u32[]{:S(2)}, u32[]{:S(2)}) %all-to-all-start.10) | async-done | bytes 786464 | tf_op jit(solution)/shard_map/all_to_all | solution.py:219
  453.2 6.2 %all-to-all-start.8 = ((bf16[2,64,3,2048]{3,0,2,1:T(2,128)(2,1)}), bf16[2,64,3,2048]{3,0,2,1:T(2,128)(2,1)S(1)}, u32[]{:S(2)}, u32[]{:S(2)}) async-start(bf16[2,64,3,2048]{3,0,2,1:T(2,128)(2,1)} %fusion.31), calls=%async_computation.9 | async-start | bytes 3145728 | tf_op jit(solution)/shard_map/all_to_all | solution.py:218
  461.9 37.3 %all-to-all-done.8 = bf16[2,64,3,2048]{3,0,2,1:T(2,128)(2,1)S(1)} async-done(((bf16[2,64,3,2048]{3,0,2,1:T(2,128)(2,1)}), bf16[2,64,3,2048]{3,0,2,1:T(2,128)(2,1)S(1)}, u32[]{:S(2)}, u32[]{:S(2)}) %all-to-all-start.8) | async-done | bytes 1572896 | tf_op jit(solution)/shard_map/all_to_all | solution.py:218
  499.2 6.1 %all-to-all-start.6 = ((bf16[3,64,2]{0,2,1:T(2,128)(2,1)}), bf16[3,64,2]{0,2,1:T(2,128)(2,1)S(1)}, u32[]{:S(2)}, u32[]{:S(2)}) async-start(bf16[3,64,2]{0,2,1:T(2,128)(2,1)} %bitcast.52), calls=%async_computation.7 | async-start | bytes 65536 | tf_op jit(solution)/shard_map/all_to_all | solution.py:232
  509.3 5.3 all-to-all-done.6
  514.5 5.4 all-to-all-start.5
  520.0 4.3 convert_multiply_fusion.6
  542.3 3.9 fusion.14
  553.3 17.8 %all-to-all-done.5 = bf16[3,128,2048]{2,0,1:T(4,128)(2,1)S(1)} async-done(((bf16[3,128,2048]{2,0,1:T(4,128)(2,1)}), bf16[3,128,2048]{2,0,1:T(4,128)(2,1)S(1)}, u32[]{:S(2)}, u32[]{:S(2)}) %all-to-all-start.5) | async-done | bytes 1572896 | tf_op jit(solution)/shard_map/all_to_all | solution.py:231
  (155 shorter events, 116.8 us)
Async XLA Ops:
  7.2 5.0 copy-start
  7.2 294.2 %all-gather.2.cloned.1.call-start = ((), (), s32[]{:S(2)}) async-start(), calls=%async_computation.12 | async-start | bytes 16220160 | tf_op jit(solution)/shard_map/all_gather | solution.py:29
  141.0 33.5 %all-to-all-start.1 = ((bf16[1,64,3,2048]{3,2,0,1:T(4,128)(2,1)}), bf16[1,64,3,2048]{3,2,0,1:T(4,128)(2,1)S(1)}, u32[]{:S(2)}, u32[]{:S(2)}) async-start(bf16[1,64,3,2048]{3,2,0,1:T(4,128)(2,1)} %bitcast.28), calls=%async_computation.1 | async-start | bytes 2097152 | tf_op jit(solution)/shard_map/all_to_all | solution.py:163
  174.4 6.5 %copy-start.7 = (bf16[1,64,3,2048]{3,2,0,1:T(4,128)(2,1)}, bf16[1,64,3,2048]{3,2,0,1:T(4,128)(2,1)S(1)}, u32[]{:S(2)}) copy-start(bf16[1,64,3,2048]{3,2,0,1:T(4,128)(2,1)S(1)} %all-to-all-done.1) | copy-start | bytes 2359300
  174.4 46.2 %all-to-all-start.3 = ((bf16[2,64,3,2048]{3,0,2,1:T(2,128)(2,1)}), bf16[2,64,3,2048]{3,0,2,1:T(2,128)(2,1)S(1)}, u32[]{:S(2)}, u32[]{:S(2)}) async-start(bf16[2,64,3,2048]{3,0,2,1:T(2,128)(2,1)} %bitcast.32), calls=%async_computation.3 | async-start | bytes 3145728 | tf_op jit(solution)/shard_map/all_to_all | solution.py:156
  220.6 34.8 %all-to-all-start.2 = ((bf16[1,64,3,2048]{3,2,0,1:T(4,128)(2,1)}), bf16[1,64,3,2048]{3,2,0,1:T(4,128)(2,1)}, u32[]{:S(2)}, u32[]{:S(2)}) async-start(bf16[1,64,3,2048]{3,2,0,1:T(4,128)(2,1)} %fusion.48), calls=%async_computation.2 | async-start | bytes 2097152 | tf_op jit(solution)/shard_map/all_to_all | solution.py:175
  255.4 46.0 %all-to-all-start.4 = ((bf16[2,64,3,2048]{3,0,2,1:T(2,128)(2,1)}), bf16[2,64,3,2048]{3,0,2,1:T(2,128)(2,1)S(1)}, u32[]{:S(2)}, u32[]{:S(2)}) async-start(bf16[2,64,3,2048]{3,0,2,1:T(2,128)(2,1)} %fusion.30), calls=%async_computation.4 | async-start | bytes 3145728 | tf_op jit(solution)/shard_map/all_to_all | solution.py:174
  261.6 197.8 %reduce-scatter.2.cloned.1.call-start = ((), (), s32[]{:S(2)}) async-start(), calls=%async_computation.13 | async-start | bytes 8355840 | tf_op jit(solution)/shard_map/reduce_scatter | solution.py:41
  301.4 7.4 %copy-start.5 = (bf16[3,512,4097]{2,1,0:T(8,128)(2,1)S(1)}, bf16[3,512,4097]{2,1,0:T(8,128)(2,1)}, u32[]{:S(2)}) copy-start(bf16[3,512,4097]{2,1,0:T(8,128)(2,1)} %all-gather.2.cloned.1.call-done) | copy-start | bytes 37757956
  304.4 4.2 copy-start.11
  304.6 7.0 %copy-start.27 = (bf16[1,512,192]{1,2,0:T(8,128)(2,1)}, bf16[1,512,192]{1,2,0:T(8,128)(2,1)S(1)}, u32[]{:S(2)}) copy-start(bf16[1,512,192]{1,2,0:T(8,128)(2,1)S(1)} %multiply_convert_fusion) | copy-start | bytes 589828
  336.2 7.4 %copy-start.32 = (bf16[1,512,192]{1,2,0:T(8,128)(2,1)S(1)}, bf16[1,512,192]{1,2,0:T(8,128)(2,1)}, u32[]{:S(2)}) copy-start(bf16[1,512,192]{1,2,0:T(8,128)(2,1)} %copy-done.31) | copy-start | bytes 589828
  337.5 34.7 %all-to-all-start.9 = ((bf16[1,64,3,2048]{3,2,0,1:T(4,128)(2,1)}), bf16[1,64,3,2048]{3,2,0,1:T(4,128)(2,1)S(1)}, u32[]{:S(2)}, u32[]{:S(2)}) async-start(bf16[1,64,3,2048]{3,2,0,1:T(4,128)(2,1)} %bitcast.59), calls=%async_computation.10 | async-start | bytes 2097152 | tf_op jit(solution)/shard_map/all_to_all | solution.py:207
  372.2 6.4 %copy-start.6 = (bf16[1,64,3,2048]{3,2,0,1:T(4,128)(2,1)}, bf16[1,64,3,2048]{3,2,0,1:T(4,128)(2,1)S(1)}, u32[]{:S(2)}) copy-start(bf16[1,64,3,2048]{3,2,0,1:T(4,128)(2,1)S(1)} %all-to-all-done.9) | copy-start | bytes 2359300
  372.2 46.0 %all-to-all-start.7 = ((bf16[2,64,3,2048]{3,0,2,1:T(2,128)(2,1)}), bf16[2,64,3,2048]{3,0,2,1:T(2,128)(2,1)S(1)}, u32[]{:S(2)}, u32[]{:S(2)}) async-start(bf16[2,64,3,2048]{3,0,2,1:T(2,128)(2,1)} %bitcast.53), calls=%async_computation.8 | async-start | bytes 3145728 | tf_op jit(solution)/shard_map/all_to_all | solution.py:200
  418.2 35.0 %all-to-all-start.10 = ((bf16[1,64,3,2048]{3,2,0,1:T(4,128)(2,1)}), bf16[1,64,3,2048]{3,2,0,1:T(4,128)(2,1)}, u32[]{:S(2)}, u32[]{:S(2)}) async-start(bf16[1,64,3,2048]{3,2,0,1:T(4,128)(2,1)} %fusion.47), calls=%async_computation.11 | async-start | bytes 2097152 | tf_op jit(solution)/shard_map/all_to_all | solution.py:219
  453.2 46.0 %all-to-all-start.8 = ((bf16[2,64,3,2048]{3,0,2,1:T(2,128)(2,1)}), bf16[2,64,3,2048]{3,0,2,1:T(2,128)(2,1)S(1)}, u32[]{:S(2)}, u32[]{:S(2)}) async-start(bf16[2,64,3,2048]{3,0,2,1:T(2,128)(2,1)} %fusion.31), calls=%async_computation.9 | async-start | bytes 3145728 | tf_op jit(solution)/shard_map/all_to_all | solution.py:218
  459.4 47.2 %slice-start = ((bf16[3,128,2049]{2,1,0:T(8,128)(2,1)}), bf16[3,128,2048]{2,1,0:T(8,128)(2,1)S(1)}, s32[]{:S(2)}) async-start(bf16[3,128,2049]{2,1,0:T(8,128)(2,1)} %reduce-scatter.2.cloned.1.call-done), calls=%async_computation.14 | async-start | bytes 3145728 | tf_op jit(solution)/shard_map/split | solution.py:42
  499.2 10.1 %copy-start.3 = (bf16[2,64,3,2048]{3,0,2,1:T(2,128)(2,1)}, bf16[2,64,3,2048]{3,0,2,1:T(2,128)(2,1)S(1)}, u32[]{:S(2)}) copy-start(bf16[2,64,3,2048]{3,0,2,1:T(2,128)(2,1)S(1)} %all-to-all-done.8) | copy-start | bytes 4718596
  499.2 15.3 %all-to-all-start.6 = ((bf16[3,64,2]{0,2,1:T(2,128)(2,1)}), bf16[3,64,2]{0,2,1:T(2,128)(2,1)S(1)}, u32[]{:S(2)}, u32[]{:S(2)}) async-start(bf16[3,64,2]{0,2,1:T(2,128)(2,1)} %bitcast.52), calls=%async_computation.7 | async-start | bytes 65536 | tf_op jit(solution)/shard_map/all_to_all | solution.py:232
  514.5 56.6 %all-to-all-start.5 = ((bf16[3,128,2048]{2,0,1:T(4,128)(2,1)}), bf16[3,128,2048]{2,0,1:T(4,128)(2,1)S(1)}, u32[]{:S(2)}, u32[]{:S(2)}) async-start(bf16[3,128,2048]{2,0,1:T(4,128)(2,1)} %copy.135), calls=%async_computation.6 | async-start | bytes 4194304 | tf_op jit(solution)/shard_map/all_to_all | solution.py:231
  542.3 3.9 copy-start.24
  542.3 3.9 copy-start.26
  552.6 20.7 %copy-start.1 = (bf16[32,2048]{1,0:T(8,128)(2,1)S(1)}, bf16[32,2048]{1,0:T(8,128)(2,1)}, u32[]{:S(2)}) copy-start(bf16[32,2048]{1,0:T(8,128)(2,1)} %param.12) | copy-start | bytes 393220
  (22 other events, 44.9 us)
Sparse Core Ops, SparseCore 0:
  136.5 120.1 all-gather.1
  333.1 66.7 reduce-scatter.1
where the time goes:
time: 591 us; the launch traced here: 581 us
  waiting for transfers between devices  259 us (44%)
  blocking collectives  113 us (19%)
  starting transfers between devices  60.8 us (10%)
  local copies, waits for them, and re-layouts  52.9 us (9%)
  matrix products  44.7 us (8%)
  other arithmetic  31.3 us (5%)
  between operations  18.5 us (3%)
    all_to_all x1, blocking collectives, in_one_piece(): lax.all_to_all(both, axis, split_axis=split_dim, concat_axis=concat_dim,...  113 us
    all_to_all x1, waiting for transfers between devices, shards(): lax.all_to_all(back_gu, 'expert', split_axis=1, concat_axis=1, tiled=True)  37.3 us
    all_to_all x1, waiting for transfers between devices, shards(): lax.all_to_all(spread_gu, 'expert', split_axis=1, concat_axis=1, tiled=True)  36.9 us
    all_to_all x1, waiting for transfers between devices, shards(): lax.all_to_all(helper_gu.reshape(2, devices, piece_rows, features), 'expe...  35.4 us
    all_to_all x1, waiting for transfers between devices, shards(): lax.all_to_all(source_gu.reshape(2, devices, piece_rows, features), 'expe...  35.4 us
    all_to_all x1, waiting for transfers between devices, shards(): lax.all_to_all(source_down.reshape(1, devices, piece_rows, features), 'ex...  23.9 us
    all_to_all x1, waiting for transfers between devices, shards(): lax.all_to_all(helper_down.reshape(1, devices, piece_rows, features), 'ex...  23.2 us
    all_to_all x1, waiting for transfers between devices, shards(): lax.all_to_all(spread_down, 'expert', split_axis=1, concat_axis=1, tiled=...  22.1 us
  transfers between devices with their start and end apart: 12, of which 10 were waited for; matrix products, arithmetic and copies ran while one was open for 13% of the time, Pallas kernels for 0%

commit v1 on v0

v1 whole, which is shorter than its diff:
```python
import functools

import jax
import jax.numpy as jnp
from jax import lax
from jax.experimental import pallas as pl
from jax.experimental.pallas import tpu as pltpu
from jax.sharding import PartitionSpec as P

LANES = 128
MIB = 1 << 20
NT = (((1,), (1,)), ((), ()))
TN = (((0,), (0,)), ((), ()))
NN = (((1,), (0,)), ((), ()))


def dot(a, b, dims):
    return lax.dot_general(a, b, dims, preferred_element_type=jnp.float32)


def iota(shape, dim):
    return lax.broadcasted_iota(jnp.int32, shape, dim)


def to_column(row):
    n = row.shape[1]
    eye = iota((n, n), 0) == iota((n, n), 1)
    return jnp.sum(jnp.where(eye, jnp.broadcast_to(row, (n, n)), 0), axis=1, keepdims=True)


def dispatch_kernel(
    chunks, devices, routing, replica, gates, host, tokens, grad_out, *outs
):
    *row_refs, picker_ref, slots_ref = outs
    topk, count = routing.shape
    features = tokens.shape[1]
    total = topk * count
    per_pair = total // devices
    part = per_pair // chunks
    host_col = to_column(host[...])
    lanes_of = iota((count, total), 1)
    rows_of = iota((total, count), 0)
    earlier = iota((count, count), 0)
    gate_at = jnp.zeros((total, count), jnp.float32)
    first_at = jnp.zeros((total, count), jnp.float32)
    picked = jnp.zeros((total, count), jnp.float32)
    picked_t = jnp.zeros((count, total), jnp.float32)
    for k in range(topk):
        expert = routing[k : k + 1, :]
        dest = lax.shift_right_logical(expert, 1)
        listed = jnp.max((host_col == expert).astype(jnp.int32), axis=0, keepdims=True)
        usable = (replica[k : k + 1, :] == 0) | (listed > 0)
        key = (1 - listed) * count + iota((1, count), 1)
        dest_col, key_col = to_column(dest), to_column(key)
        ahead = (dest_col == dest) & (key_col < key)
        rank = jnp.sum(ahead.astype(jnp.int32), axis=0, keepdims=True)
        slot = (rank // part) * (devices * part) + dest * part + rank % part
        slot = jnp.where(usable, slot, -1)
        slots_ref[k : k + 1, :] = slot
        match = rows_of == slot
        picked = jnp.where(match, 1.0, picked)
        gate_at = jnp.where(match, gates[k : k + 1, :], gate_at)
        first_at = jnp.where(match, listed.astype(jnp.float32), first_at)
        picked_t = jnp.where(lanes_of == to_column(slot), 1.0, picked_t)
    picker_ref[...] = picked_t.astype(jnp.bfloat16)
    any_row = jnp.sum(picked, axis=1, keepdims=True)
    gate = jnp.sum(gate_at, axis=1, keepdims=True)
    first = jnp.sum(first_at, axis=1, keepdims=True)
    second = any_row - first
    lane = iota((total, LANES), 1)
    meta = jnp.where(lane == 0, gate * first, 0.0)
    meta = jnp.where(lane == 1, gate * second, meta)
    meta = jnp.where(lane == 2, first, meta)
    meta = jnp.where(lane == 3, second, meta).astype(jnp.bfloat16)
    picker = picked.astype(jnp.bfloat16)
    size = total // chunks
    for c, out in enumerate(row_refs):
        mine = slice(c * size, (c + 1) * size)
        out[:, :features] = dot(picker[mine], tokens[...], NN).astype(jnp.bfloat16)
        out[:, features : 2 * features] = dot(picker[mine], grad_out[...], NN).astype(jnp.bfloat16)
        out[:, 2 * features :] = meta[mine]


def pieces_of(refs, start, size, cols):
    got, at = [], 0
    for r in refs:
        low, high = max(start, at), min(start + size, at + r.shape[0])
        if low < high:
            got.append(r[low - at : high - at, cols])
        at += r.shape[0]
    return got[0] if len(got) == 1 else jnp.concatenate(got, axis=0)


def put_pieces(refs, start, cols, value):
    at = 0
    for r in refs:
        low, high = max(start, at), min(start + value.shape[0], at + r.shape[0])
        if low < high:
            r[low - at : high - at, cols] = value[low - start : high - start]
        at += r.shape[0]


def expert_kernel(experts, n_in, n_out, order, *refs):
    pieces = refs[:n_in]
    gu = refs[n_in : n_in + experts]
    down = refs[n_in + experts : n_in + 2 * experts]
    outs = refs[n_in + 2 * experts : n_in + 2 * experts + n_out]
    gm_ref, hg_ref = refs[n_in + 2 * experts + n_out :]
    quarter, features = down[0].shape[1:]
    width = experts * quarter
    rows = sum(p.shape[0] for p in pieces)
    block = min(rows, 256)

    def stack(parts):
        return parts[0] if experts == 1 else jnp.concatenate(parts, axis=0)

    w_gate = stack([w[0, 0] for w in gu])
    w_up = stack([w[0, 1] for w in gu])
    w_down = stack([w[0] for w in down])
    for at in range(0, rows, block):
        x = pieces_of(pieces, at, block, slice(0, features))
        dy = pieces_of(pieces, at, block, slice(features, 2 * features))
        meta = pieces_of(pieces, at, block, slice(2 * features, 2 * features + LANES)).astype(jnp.float32)
        weight, live = meta[:, 0:1], meta[:, 2:3]
        if experts == 2:
            is_first = iota((block, width), 1) < quarter
            weight = jnp.where(is_first, weight, meta[:, 1:2])
            live = jnp.where(is_first, live, meta[:, 3:4])
        gate = dot(x, w_gate, NT)
        up = dot(x, w_up, NT)
        back = dot(dy, w_down, NT)
        s = jax.nn.sigmoid(gate)
        active = gate * s
        hidden = (active * up).astype(jnp.bfloat16).astype(jnp.float32)
        dg = jnp.sum(hidden * back * live, axis=1, keepdims=True)
        grad_hidden = back * weight
        gm_gate = (grad_hidden * up * s * (1.0 + gate * (1.0 - s))).astype(jnp.bfloat16)
        gm_up = (grad_hidden * active).astype(jnp.bfloat16)
        gm_ref[at : at + block, :width] = gm_gate
        gm_ref[at : at + block, width:] = gm_up
        hg_ref[at : at + block] = (hidden * weight).astype(jnp.bfloat16)
        dx = dot(gm_gate, w_gate, NN) + dot(gm_up, w_up, NN)
        put_pieces(outs, at, slice(0, features), dx.astype(jnp.bfloat16))
        put_pieces(
            outs,
            at,
            slice(features, features + LANES),
            jnp.broadcast_to(dg, (block, LANES)).astype(jnp.bfloat16),
        )


def weights_kernel(n, order, *refs):
    x0, x1, dy0, dy1 = (refs[i * n : (i + 1) * n] for i in range(4))
    gm0, hg0, gm1, hg1, out_gu, out_down = refs[4 * n :]
    q = hg0.shape[1]
    first = order[0]
    second = 1 - first

    def whole(parts):
        return jnp.concatenate([p[...] for p in parts], axis=0)

    a = dot(gm0[...], whole(x0), TN)
    b = dot(gm1[...], whole(x1), TN)
    for j in range(2):
        out_gu[first, j] = (a[j * q : (j + 1) * q] + b[2 * j * q : (2 * j + 1) * q]).astype(jnp.bfloat16)
        out_gu[second, j] = b[(2 * j + 1) * q : (2 * j + 2) * q].astype(jnp.bfloat16)
    a = dot(hg0[...], whole(dy0), TN)
    b = dot(hg1[...], whole(dy1), TN)
    out_down[first] = (a + b[:q]).astype(jnp.bfloat16)
    out_down[second] = b[q:].astype(jnp.bfloat16)


def home_kernel(chunks, picker, slots, *refs):
    rows, (tok_ref, gate_ref) = refs[:chunks], refs[chunks:]
    features = tok_ref.shape[1]
    topk, count = slots.shape
    size = rows[0].shape[0]
    total = jnp.zeros((count, features), jnp.float32)
    for c, r in enumerate(rows):
        total += dot(picker[:, c * size : (c + 1) * size], r[:, :features], NN)
    tok_ref[...] = total.astype(jnp.bfloat16)
    dg = jnp.concatenate([r[:, features : features + LANES] for r in rows], axis=0).astype(jnp.float32)[:, :1]
    rows_of = iota((chunks * size, count), 0)
    for k in range(topk):
        match = rows_of == slots[k : k + 1, :]
        gate_ref[k : k + 1, :] = jnp.sum(jnp.where(match, dg, 0.0), axis=0, keepdims=True)


def shift(x, step):
    n = lax.axis_size("dp")
    return lax.ppermute(x, "dp", [(i, (i + step) % n) for i in range(n)])


def spread(x):
    half = x.shape[0] // 2
    left, right = shift(x, 1), shift(x, -1)
    return (x, left, right, shift(left[:half], 1), shift(right[half:], -1))


def add(a, b):
    return (a.astype(jnp.float32) + b.astype(jnp.float32)).astype(jnp.bfloat16)


def collect(own, left1, left2, right1, right2, far1, far2):
    from_left1 = shift(add(right1, shift(far1, 1)), 1)
    from_left2 = shift(right2, 1)
    from_right1 = shift(left1, -1)
    from_right2 = shift(add(left2, shift(far2, -1)), -1)
    total = own.astype(jnp.float32)
    total += jnp.concatenate([from_left1, from_left2], axis=0).astype(jnp.float32)
    total += jnp.concatenate([from_right1, from_right2], axis=0).astype(jnp.float32)
    return total.astype(jnp.bfloat16)


def exchange(x):
    return lax.all_to_all(x, "expert", split_axis=0, concat_axis=0, tiled=True)


def shards(tokens, grad_out, routing, replica, gates, host_expert, w_gate_up, w_down):
    devices = lax.axis_size("expert")
    device_id = lax.axis_index("expert")
    count, features = tokens.shape
    topk = routing.shape[1]
    owned, quarter = w_down.shape[:2]
    chunks = 2
    total = count * topk
    size = total // chunks
    wide = 2 * features + LANES
    bf16 = jnp.bfloat16

    first = jnp.sum(jnp.where(host_expert // owned == device_id, host_expert % owned, 0))
    order = first.astype(jnp.int32).reshape(1)

    *sent, picker, slots = pl.pallas_call(
        functools.partial(dispatch_kernel, chunks, devices),
        out_shape=[jax.ShapeDtypeStruct((size, wide), bf16)] * chunks
        + [
            jax.ShapeDtypeStruct((count, total), bf16),
            jax.ShapeDtypeStruct((topk, count), jnp.int32),
        ],
        compiler_params=pltpu.CompilerParams(vmem_limit_bytes=32 * MIB),
        name="dispatch",
    )(routing.T, replica.T, gates.T.astype(jnp.float32), host_expert.reshape(1, devices), tokens, grad_out)

    pieces = [spread(exchange(s)) for s in sent]
    half = size // 2

    def experts_of(c, experts):
        parts = pieces[c]
        rows = sum(p.shape[0] for p in parts)
        width = experts * quarter
        heights = [size] + [half] * 6
        gu_spec = [
            pl.BlockSpec((1, 2, quarter, features), lambda i, o, e=e: ((1 - 2 * e) * o[0] + e, 0, 0, 0))
            for e in range(experts)
        ]
        down_spec = [
            pl.BlockSpec((1, quarter, features), lambda i, o, e=e: ((1 - 2 * e) * o[0] + e, 0, 0))
            for e in range(experts)
        ]
        full = lambda h, w: pl.BlockSpec((h, w), lambda i, o: (0, 0))
        return pl.pallas_call(
            functools.partial(expert_kernel, experts, len(parts), len(heights)),
            grid_spec=pltpu.PrefetchScalarGridSpec(
                num_scalar_prefetch=1,
                grid=(1,),
                in_specs=[full(*p.shape) for p in parts] + gu_spec + down_spec,
                out_specs=[full(h, features + LANES) for h in heights]
                + [full(rows, 2 * width), full(rows, width)],
            ),
            out_shape=[jax.ShapeDtypeStruct((h, features + LANES), bf16) for h in heights]
            + [
                jax.ShapeDtypeStruct((rows, 2 * width), bf16),
                jax.ShapeDtypeStruct((rows, width), bf16),
            ],
            compiler_params=pltpu.CompilerParams(vmem_limit_bytes=48 * MIB),
            name=f"experts_{experts}",
        )(order, *parts, *[w_gate_up] * experts, *[w_down] * experts)

    *dx0, gm0, hg0 = experts_of(0, 1)
    *dx1, gm1, hg1 = experts_of(1, 2)

    steps = 4
    cut = features // steps
    n = len(pieces[0])
    x_spec = [pl.BlockSpec((p.shape[0], cut), lambda i, o: (0, i)) for p in pieces[0]]
    dy_spec = [pl.BlockSpec((p.shape[0], cut), lambda i, o: (0, i + steps)) for p in pieces[0]]
    full = lambda a: pl.BlockSpec(a.shape, lambda i, o: (0, 0))
    grad_gu, grad_down = pl.pallas_call(
        functools.partial(weights_kernel, n),
        grid_spec=pltpu.PrefetchScalarGridSpec(
            num_scalar_prefetch=1,
            grid=(steps,),
            in_specs=x_spec * 2 + dy_spec * 2 + [full(a) for a in (gm0, hg0, gm1, hg1)],
            out_specs=[
                pl.BlockSpec((owned, 2, quarter, cut), lambda i, o: (0, 0, 0, i)),
                pl.BlockSpec((owned, quarter, cut), lambda i, o: (0, 0, i)),
            ],
        ),
        out_shape=[
            jax.ShapeDtypeStruct(w_gate_up.shape, bf16),
            jax.ShapeDtypeStruct(w_down.shape, bf16),
        ],
        compiler_params=pltpu.CompilerParams(vmem_limit_bytes=40 * MIB),
        name="weights",
    )(order, *pieces[0], *pieces[1], *pieces[0], *pieces[1], gm0, hg0, gm1, hg1)

    home = [exchange(collect(*dx)) for dx in (dx0, dx1)]
    grad_tokens, grad_gates = pl.pallas_call(
        functools.partial(home_kernel, chunks),
        out_shape=[
            jax.ShapeDtypeStruct((count, features), bf16),
            jax.ShapeDtypeStruct((topk, count), jnp.float32),
        ],
        compiler_params=pltpu.CompilerParams(vmem_limit_bytes=16 * MIB),
        name="home",
    )(picker, slots, *home)
    return grad_tokens, grad_gates.T, grad_gu, grad_down


def solution(mesh):
    in_specs = (
        P(("dp", "expert"), None),
        P(("dp", "expert"), None),
        P(("dp", "expert"), None),
        P(("dp", "expert"), None),
        P(("dp", "expert"), None),
        P(),
        P("expert", None, "dp", None),
        P("expert", "dp", None),
    )
    out_specs = (
        P(("dp", "expert"), None),
        P(("dp", "expert"), None),
        P("expert", None, "dp", None),
        P("expert", "dp", None),
    )
    return jax.shard_map(shards, mesh=mesh, in_specs=in_specs, out_specs=out_specs, check_vma=False)
```

time: 591 us -> 232 us (0.39); the launches traced: 581 us -> 231 us
  waiting for transfers between devices: 259 us -> 110 us
  blocking collectives: 113 us -> 0 us
  matrix products: 44.7 us -> 0 us
  Pallas kernels: 0 us -> 28.1 us
  local copies, waits for them, and re-layouts: 52.9 us -> 26.4 us
  other arithmetic: 31.3 us -> 6.54 us
  between operations: 18.5 us -> 0.84 us
    all_to_all x10 -> x4, waiting for transfers between devices: 259 us -> 61.2 us  [exchange(): return lax.all_to_all(x, 'expert', split_axis=0, concat_axis=0, tiled=True)]
    all_to_all x1 -> x0, blocking collectives: 113 us -> none  [in_one_piece(): lax.all_to_all(both, axis, split_axis=split_dim, concat_axis=concat_dim,...]
    ppermute x0 -> x20, waiting for transfers between devices: none -> 48.9 us  [shift(): return lax.ppermute(x, 'dp', [(i, (i + step) % n) for i in range(n)])]
    dot_general x21 -> x0, matrix products: 44.7 us -> none  [the longest x3 10.3 us: expert_block(): jnp.einsum('jrf,rd->jfd', grad_mixed, inputs, preferred_element_type=jnp....]
    pallas_call x0 -> x5, Pallas kernels: none -> 28.1 us  [the longest x2 17.4 us: experts_of(): pl.pallas_call(functools.partial(expert_kernel, experts, len(parts), len(...]
    all_to_all x10 -> x4, starting transfers between devices: 60.7 us -> 39.7 us  [exchange(): return lax.all_to_all(x, 'expert', split_axis=0, concat_axis=0, tiled=True)]
    ppermute x0 -> x20, starting transfers between devices: none -> 19.3 us  [shift(): return lax.ppermute(x, 'dp', [(i, (i + step) % n) for i in range(n)])]
    gather x4 -> x0, local copies, waits for them, and re-layouts: 12.8 us -> none  [the longest x1 3.71 us: shards(): spread_gu = jnp.take(spread_gu, owner_of_helper, axis=1)]
  transfers between devices with their start and end apart: 12 -> 24, of which waited for: 10 -> 10; matrix products, arithmetic and copies ran while one was open for 13% -> 4% of each run, Pallas kernels for 0% -> 11%
where the time goes in v1:
time: 232 us; the launch traced here: 231 us
  waiting for transfers between devices  110 us (47%)
  starting transfers between devices  59 us (25%)
  Pallas kernels  28.1 us (12%)
  local copies, waits for them, and re-layouts  26.4 us (11%)
  other arithmetic  6.54 us (3%)
    all_to_all x4, waiting for transfers between devices, exchange(): return lax.all_to_all(x, 'expert', split_axis=0, concat_axis=0, tiled=True)  61.2 us
    ppermute x20, waiting for transfers between devices, shift(): return lax.ppermute(x, 'dp', [(i, (i + step) % n) for i in range(n)])  48.9 us
    all_to_all x4, starting transfers between devices, exchange(): return lax.all_to_all(x, 'expert', split_axis=0, concat_axis=0, tiled=True)  39.7 us
    ppermute x20, starting transfers between devices, shift(): return lax.ppermute(x, 'dp', [(i, (i + step) % n) for i in range(n)])  19.3 us
    pallas_call x2, Pallas kernels, experts_of(): pl.pallas_call(functools.partial(expert_kernel, experts, len(parts), len(...  17.4 us
    all_to_all x8, local copies, waits for them, and re-layouts, exchange(): return lax.all_to_all(x, 'expert', split_axis=0, concat_axis=0, tiled=True)  11.1 us
    unnamed x40, local copies, waits for them, and re-layouts  10.7 us
    pallas_call x1, Pallas kernels, shards(): pl.pallas_call(functools.partial(weights_kernel, n), grid_spec=pltpu.Pref...  8.5 us
  transfers between devices with their start and end apart: 24, of which 10 were waited for; matrix products, arithmetic and copies ran while one was open for 4% of the time, Pallas kernels for 11%

profile of v1, /device:TPU:1, one launch (start us, length us, event | category | flops | bytes accessed | tf_op | source)
XLA Modules:
  0.0 231.0 jit_solution(1549269306428453473)
XLA Ops:
  7.6 13.0 %all-to-all-start = ((bf16[64,2,4224]{2,1,0:T(2,128)(2,1)}), bf16[64,2,4224]{2,1,0:T(2,128)(2,1)S(1)}, u32[]{:S(2)}, u32[]{:S(2)}) async-start(bf16[64,2,4224]{2,1,0:T(2,128)(2,1)} %all_to_all.28), calls=%async_computation | async-start | bytes 2162688 | tf_op jit(solution)/shard_map/all_to_all | solution.py:216
  21.9 28.0 %all-to-all-done = bf16[64,2,4224]{2,1,0:T(2,128)(2,1)S(1)} async-done(((bf16[64,2,4224]{2,1,0:T(2,128)(2,1)}), bf16[64,2,4224]{2,1,0:T(2,128)(2,1)S(1)}, u32[]{:S(2)}, u32[]{:S(2)}) %all-to-all-start) | async-done | bytes 1081376 | tf_op jit(solution)/shard_map/all_to_all | solution.py:216
  49.9 6.4 %all-to-all-start.2 = ((bf16[64,2,4224]{2,1,0:T(2,128)(2,1)}), bf16[64,2,4224]{2,1,0:T(2,128)(2,1)}, u32[]{:S(2)}, u32[]{:S(2)}) async-start(bf16[64,2,4224]{2,1,0:T(2,128)(2,1)} %all_to_all.34), calls=%async_computation.2 | async-start | bytes 2162688 | tf_op jit(solution)/shard_map/all_to_all | solution.py:216
  59.6 25.8 %all-to-all-done.2 = bf16[64,2,4224]{2,1,0:T(2,128)(2,1)} async-done(((bf16[64,2,4224]{2,1,0:T(2,128)(2,1)}), bf16[64,2,4224]{2,1,0:T(2,128)(2,1)}, u32[]{:S(2)}, u32[]{:S(2)}) %all-to-all-start.2) | async-done | bytes 1081376 | tf_op jit(solution)/shard_map/all_to_all | solution.py:216
  90.7 1.9 slice.17
  92.6 2.7 %collective-permute-start.3 = (bf16[64,4224]{1,0:T(8,128)(2,1)}, bf16[64,4224]{1,0:T(8,128)(2,1)}, u32[]{:S(2)}, u32[]{:S(2)}) collective-permute-start(bf16[64,4224]{1,0:T(8,128)(2,1)} %slice.17), channel_id=1, source_target_pairs={{0,192},{64,0},{128,64},{192,128},{1,193},{65,1},{129,65},{193,129... | collective-permute-start | bytes 1622024 | tf_op jit(solution)/shard_map/ppermute | solution.py:191
  95.3 18.5 %collective-permute-done.10.refs_1_.refs_6_.refs_16_ = bf16[128,4224]{1,0:T(8,128)(2,1)S(1)} collective-permute-done((bf16[128,4224]{1,0:T(8,128)(2,1)S(1)}, bf16[128,4224]{1,0:T(8,128)(2,1)S(1)}, u32[]{:S(2)}, u32[]{:S(2)}) %collective-permute-start.10) | collective-permute-done | bytes 1081376 | tf_op jit(solution)/shard_map/ppermute | solution.py:191
  116.1 2.4 %collective-permute-start.13 = (bf16[64,4224]{1,0:T(8,128)(2,1)}, bf16[64,4224]{1,0:T(8,128)(2,1)}, u32[]{:S(2)}, u32[]{:S(2)}) collective-permute-start(bf16[64,4224]{1,0:T(8,128)(2,1)} %slice.19), channel_id=1, source_target_pairs={{0,192},{64,0},{128,64},{192,128},{1,193},{65,1},{129,65},{193,129... | collective-permute-start | bytes 1622024 | tf_op jit(solution)/shard_map/ppermute | solution.py:191
  119.2 6.3 %collective-permute-done.2.refs_3_.refs_13_ = bf16[64,4224]{1,0:T(8,128)(2,1)} collective-permute-done((bf16[64,4224]{1,0:T(8,128)(2,1)}, bf16[64,4224]{1,0:T(8,128)(2,1)}, u32[]{:S(2)}, u32[]{:S(2)}) %collective-permute-start.2) | collective-permute-done | bytes 540704 | tf_op jit(solution)/shard_map/ppermute | solution.py:191
  125.5 6.6 %experts_1.1 = (bf16[128,2176]{1,0:T(8,128)(2,1)S(1)}, bf16[64,2176]{1,0:T(8,128)(2,1)S(1)}, bf16[64,2176]{1,0:T(8,128)(2,1)S(1)}, bf16[64,2176]{1,0:T(8,128)(2,...) custom-call(s32[1]{0:T(128)} %bitcast.4.order, ...), custom_call_target="tpu_custom_call" | custom-call | tf_op jit(solution)/shard_map/experts_1/pallas_call | solution.py:262
  134.8 1.7 collective-permute-start.8
  138.5 10.8 %experts_2.1 = (bf16[128,2176]{1,0:T(8,128)(2,1)S(1)}, bf16[64,2176]{1,0:T(8,128)(2,1)}, bf16[64,2176]{1,0:T(8,128)(2,1)S(1)}, bf16[64,2176]{1,0:T(8,128)(2,1)S(...) custom-call(s32[1]{0:T(128)} %bitcast.4.order, ...), custom_call_target="tpu_custom_call" | custom-call | tf_op jit(solution)/shard_map/experts_2/pallas_call | solution.py:262
  150.0 1.5 collective-permute-start.5
  151.6 11.7 %collective-permute-done.14 = bf16[64,2176]{1,0:T(8,128)(2,1)S(1)} collective-permute-done((bf16[64,2176]{1,0:T(8,128)(2,1)S(1)}, bf16[64,2176]{1,0:T(8,128)(2,1)S(1)}, u32[]{:S(2)}, u32[]{:S(2)}) %collective-permute-start.14) | collective-permute-done | bytes 278560 | tf_op jit(solution)/shard_map/ppermute | solution.py:191
  164.4 4.9 %collective-permute-done.5 = bf16[64,2176]{1,0:T(8,128)(2,1)S(1)} collective-permute-done((bf16[64,2176]{1,0:T(8,128)(2,1)S(1)}, bf16[64,2176]{1,0:T(8,128)(2,1)S(1)}, u32[]{:S(2)}, u32[]{:S(2)}) %collective-permute-start.5) | collective-permute-done | bytes 278560 | tf_op jit(solution)/shard_map/ppermute | solution.py:191
  170.4 2.1 all_to_all.31
  172.4 13.7 %all-to-all-start.1 = ((bf16[64,2,2176]{2,1,0:T(2,128)(2,1)}), bf16[64,2,2176]{2,1,0:T(2,128)(2,1)}, u32[]{:S(2)}, u32[]{:S(2)}) async-start(bf16[64,2,2176]{2,1,0:T(2,128)(2,1)} %all_to_all.31), calls=%async_computation.1 | async-start | bytes 1114112 | tf_op jit(solution)/shard_map/all_to_all | solution.py:216
  188.3 6.8 %collective-permute-done.19 = bf16[64,2176]{1,0:T(8,128)(2,1)S(1)} collective-permute-done((bf16[64,2176]{1,0:T(8,128)(2,1)S(1)}, bf16[64,2176]{1,0:T(8,128)(2,1)S(1)}, u32[]{:S(2)}, u32[]{:S(2)}) %collective-permute-start.19) | collective-permute-done | bytes 278560 | tf_op jit(solution)/shard_map/ppermute | solution.py:191
  195.1 2.1 add_convert_fusion
  197.3 2.1 all_to_all.37
  199.4 4.7 %all-to-all-done.1 = bf16[64,2,2176]{2,1,0:T(2,128)(2,1)} async-done(((bf16[64,2,2176]{2,1,0:T(2,128)(2,1)}), bf16[64,2,2176]{2,1,0:T(2,128)(2,1)}, u32[]{:S(2)}, u32[]{:S(2)}) %all-to-all-start.1) | async-done | bytes 557088 | tf_op jit(solution)/shard_map/all_to_all | solution.py:216
  204.1 6.7 %all-to-all-start.3 = ((bf16[64,2,2176]{2,1,0:T(2,128)(2,1)}), bf16[64,2,2176]{2,1,0:T(2,128)(2,1)}, u32[]{:S(2)}, u32[]{:S(2)}) async-start(bf16[64,2,2176]{2,1,0:T(2,128)(2,1)} %all_to_all.37), calls=%async_computation.3 | async-start | bytes 1114112 | tf_op jit(solution)/shard_map/all_to_all | solution.py:216
  216.4 8.5 %weights.1 = (bf16[2,2,192,2048]{3,2,1,0:T(8,128)(2,1)}, bf16[2,192,2048]{2,1,0:T(8,128)(2,1)}) custom-call(s32[1]{0:T(128)} %bitcast.4.order, bf16[128,4224]{1,0:T(8,128)(2,1)S(1)} %all_to_all.30.refs_0_.refs_10_, bf16[128,4224]{1,0:T(8,128)(2,1)S(1)} %collective-permute-done.refs_1_.refs_11_, bf16[128,4224]{1,0:T(8,128)(2,1)} %collective-permute-done.1.refs_2_.refs_12_, ...), custom_call_target="tpu_custom_call" | custom-call | tf_op jit(solution)/shard_map/weights/pallas_call | solution.py:289
  226.2 2.6 %all-to-all-done.3 = bf16[64,2,2176]{2,1,0:T(2,128)(2,1)} async-done(((bf16[64,2,2176]{2,1,0:T(2,128)(2,1)}), bf16[64,2,2176]{2,1,0:T(2,128)(2,1)}, u32[]{:S(2)}, u32[]{:S(2)}) %all-to-all-start.3) | async-done | bytes 557088 | tf_op jit(solution)/shard_map/all_to_all | solution.py:216
  (89 shorter events, 38.6 us)
Async XLA Ops:
  7.6 42.2 %all-to-all-start = ((bf16[64,2,4224]{2,1,0:T(2,128)(2,1)}), bf16[64,2,4224]{2,1,0:T(2,128)(2,1)S(1)}, u32[]{:S(2)}, u32[]{:S(2)}) async-start(bf16[64,2,4224]{2,1,0:T(2,128)(2,1)} %all_to_all.28), calls=%async_computation | async-start | bytes 2162688 | tf_op jit(solution)/shard_map/all_to_all | solution.py:216
  49.9 35.6 %all-to-all-start.2 = ((bf16[64,2,4224]{2,1,0:T(2,128)(2,1)}), bf16[64,2,4224]{2,1,0:T(2,128)(2,1)}, u32[]{:S(2)}, u32[]{:S(2)}) async-start(bf16[64,2,4224]{2,1,0:T(2,128)(2,1)} %all_to_all.34), calls=%async_computation.2 | async-start | bytes 2162688 | tf_op jit(solution)/shard_map/all_to_all | solution.py:216
  56.7 33.1 %collective-permute-start = (bf16[128,4224]{1,0:T(8,128)(2,1)S(1)}, bf16[128,4224]{1,0:T(8,128)(2,1)S(1)}, u32[]{:S(2)}, u32[]{:S(2)}) collective-permute-start(bf16[128,4224]{1,0:T(8,128)(2,1)S(1)} %all_to_all.30.refs_0_.refs_10_), channel_id=1, source_target_pairs={{0,64},{64,128},{128,192},{192,0},{1,65},{65,129},{129,193},{193,1... | collective-permute-start | bytes 3244040 | tf_op jit(solution)/shard_map/ppermute | solution.py:191
  58.1 32.6 %collective-permute-start.1 = (bf16[128,4224]{1,0:T(8,128)(2,1)S(1)}, bf16[128,4224]{1,0:T(8,128)(2,1)}, u32[]{:S(2)}, u32[]{:S(2)}) collective-permute-start(bf16[128,4224]{1,0:T(8,128)(2,1)S(1)} %all_to_all.30.refs_0_.refs_10_), channel_id=1, source_target_pairs={{0,192},{64,0},{128,64},{192,128},{1,193},{65,1},{129,65},{193,129... | collective-permute-start | bytes 3244040 | tf_op jit(solution)/shard_map/ppermute | solution.py:191
  86.9 26.9 %collective-permute-start.10 = (bf16[128,4224]{1,0:T(8,128)(2,1)S(1)}, bf16[128,4224]{1,0:T(8,128)(2,1)S(1)}, u32[]{:S(2)}, u32[]{:S(2)}) collective-permute-start(bf16[128,4224]{1,0:T(8,128)(2,1)S(1)} %all_to_all.36.refs_0_.refs_5_.refs_15_), channel_id=1, source_target_pairs={{0,64},{64,128},{128,192},{192,0},{1,65},{65,129},{129,193},{193,1... | collective-permute-start | bytes 3244040 | tf_op jit(solution)/shard_map/ppermute | solution.py:191
  88.3 26.4 %collective-permute-start.11 = (bf16[128,4224]{1,0:T(8,128)(2,1)S(1)}, bf16[128,4224]{1,0:T(8,128)(2,1)S(1)}, u32[]{:S(2)}, u32[]{:S(2)}) collective-permute-start(bf16[128,4224]{1,0:T(8,128)(2,1)S(1)} %all_to_all.36.refs_0_.refs_5_.refs_15_), channel_id=1, source_target_pairs={{0,192},{64,0},{128,64},{192,128},{1,193},{65,1},{129,65},{193,129... | collective-permute-start | bytes 3244040 | tf_op jit(solution)/shard_map/ppermute | solution.py:191
  90.7 34.8 %collective-permute-start.2 = (bf16[64,4224]{1,0:T(8,128)(2,1)}, bf16[64,4224]{1,0:T(8,128)(2,1)}, u32[]{:S(2)}, u32[]{:S(2)}) collective-permute-start(bf16[64,4224]{1,0:T(8,128)(2,1)} %slice.16), channel_id=1, source_target_pairs={{0,64},{64,128},{128,192},{192,0},{1,65},{65,129},{129,193},{193,1... | collective-permute-start | bytes 1622024 | tf_op jit(solution)/shard_map/ppermute | solution.py:191
  92.6 32.9 %collective-permute-start.3 = (bf16[64,4224]{1,0:T(8,128)(2,1)}, bf16[64,4224]{1,0:T(8,128)(2,1)}, u32[]{:S(2)}, u32[]{:S(2)}) collective-permute-start(bf16[64,4224]{1,0:T(8,128)(2,1)} %slice.17), channel_id=1, source_target_pairs={{0,192},{64,0},{128,64},{192,128},{1,193},{65,1},{129,65},{193,129... | collective-permute-start | bytes 1622024 | tf_op jit(solution)/shard_map/ppermute | solution.py:191
  114.7 22.4 %collective-permute-start.12 = (bf16[64,4224]{1,0:T(8,128)(2,1)}, bf16[64,4224]{1,0:T(8,128)(2,1)}, u32[]{:S(2)}, u32[]{:S(2)}) collective-permute-start(bf16[64,4224]{1,0:T(8,128)(2,1)} %slice.18), channel_id=1, source_target_pairs={{0,64},{64,128},{128,192},{192,0},{1,65},{65,129},{129,193},{193,1... | collective-permute-start | bytes 1622024 | tf_op jit(solution)/shard_map/ppermute | solution.py:191
  116.1 22.3 %collective-permute-start.13 = (bf16[64,4224]{1,0:T(8,128)(2,1)}, bf16[64,4224]{1,0:T(8,128)(2,1)}, u32[]{:S(2)}, u32[]{:S(2)}) collective-permute-start(bf16[64,4224]{1,0:T(8,128)(2,1)} %slice.19), channel_id=1, source_target_pairs={{0,192},{64,0},{128,64},{192,128},{1,193},{65,1},{129,65},{193,129... | collective-permute-start | bytes 1622024 | tf_op jit(solution)/shard_map/ppermute | solution.py:191
  132.9 16.5 %collective-permute-start.4 = (bf16[64,2176]{1,0:T(8,128)(2,1)S(1)}, bf16[64,2176]{1,0:T(8,128)(2,1)S(1)}, u32[]{:S(2)}, u32[]{:S(2)}) collective-permute-start(bf16[64,2176]{1,0:T(8,128)(2,1)S(1)} %get-tuple-element.35), channel_id=1, source_target_pairs={{0,64},{64,128},{128,192},{192,0},{1,65},{65,129},{129,193},{193,1... | collective-permute-start | bytes 835592 | tf_op jit(solution)/shard_map/ppermute | solution.py:191
  133.8 30.4 %collective-permute-start.6 = (bf16[64,2176]{1,0:T(8,128)(2,1)S(1)}, bf16[64,2176]{1,0:T(8,128)(2,1)S(1)}, u32[]{:S(2)}, u32[]{:S(2)}) collective-permute-start(bf16[64,2176]{1,0:T(8,128)(2,1)S(1)} %get-tuple-element.36), channel_id=1, source_target_pairs={{0,64},{64,128},{128,192},{192,0},{1,65},{65,129},{129,193},{193,1... | collective-permute-start | bytes 835592 | tf_op jit(solution)/shard_map/ppermute | solution.py:191
  134.8 15.1 %collective-permute-start.8 = (bf16[64,2176]{1,0:T(8,128)(2,1)S(1)}, bf16[64,2176]{1,0:T(8,128)(2,1)S(1)}, u32[]{:S(2)}, u32[]{:S(2)}) collective-permute-start(bf16[64,2176]{1,0:T(8,128)(2,1)S(1)} %get-tuple-element.39), channel_id=1, source_target_pairs={{0,192},{64,0},{128,64},{192,128},{1,193},{65,1},{129,65},{193,129... | collective-permute-start | bytes 835592 | tf_op jit(solution)/shard_map/ppermute | solution.py:191
  137.1 27.2 %collective-permute-start.7 = (bf16[64,2176]{1,0:T(8,128)(2,1)S(1)}, bf16[64,2176]{1,0:T(8,128)(2,1)S(1)}, u32[]{:S(2)}, u32[]{:S(2)}) collective-permute-start(bf16[64,2176]{1,0:T(8,128)(2,1)S(1)} %get-tuple-element.37), channel_id=1, source_target_pairs={{0,192},{64,0},{128,64},{192,128},{1,193},{65,1},{129,65},{193,129... | collective-permute-start | bytes 835592 | tf_op jit(solution)/shard_map/ppermute | solution.py:191
  149.3 39.0 %collective-permute-start.16 = (bf16[64,2176]{1,0:T(8,128)(2,1)}, bf16[64,2176]{1,0:T(8,128)(2,1)}, u32[]{:S(2)}, u32[]{:S(2)}) collective-permute-start(bf16[64,2176]{1,0:T(8,128)(2,1)} %get-tuple-element.44), channel_id=1, source_target_pairs={{0,64},{64,128},{128,192},{192,0},{1,65},{65,129},{129,193},{193,1... | collective-permute-start | bytes 835592 | tf_op jit(solution)/shard_map/ppermute | solution.py:191
  149.4 13.9 %collective-permute-start.14 = (bf16[64,2176]{1,0:T(8,128)(2,1)S(1)}, bf16[64,2176]{1,0:T(8,128)(2,1)S(1)}, u32[]{:S(2)}, u32[]{:S(2)}) collective-permute-start(bf16[64,2176]{1,0:T(8,128)(2,1)S(1)} %get-tuple-element.43), channel_id=1, source_target_pairs={{0,64},{64,128},{128,192},{192,0},{1,65},{65,129},{129,193},{193,1... | collective-permute-start | bytes 835592 | tf_op jit(solution)/shard_map/ppermute | solution.py:191
  150.0 19.3 %collective-permute-start.5 = (bf16[64,2176]{1,0:T(8,128)(2,1)S(1)}, bf16[64,2176]{1,0:T(8,128)(2,1)S(1)}, u32[]{:S(2)}, u32[]{:S(2)}) collective-permute-start(bf16[64,2176]{1,0:T(8,128)(2,1)S(1)} %add_convert_fusion.5), channel_id=1, source_target_pairs={{0,64},{64,128},{128,192},{192,0},{1,65},{65,129},{129,193},{193,1... | collective-permute-start | bytes 835592 | tf_op jit(solution)/shard_map/ppermute | solution.py:191
  163.3 6.0 %collective-permute-start.9 = (bf16[64,2176]{1,0:T(8,128)(2,1)S(1)}, bf16[64,2176]{1,0:T(8,128)(2,1)S(1)}, u32[]{:S(2)}, u32[]{:S(2)}) collective-permute-start(bf16[64,2176]{1,0:T(8,128)(2,1)S(1)} %add_convert_fusion.4), channel_id=1, source_target_pairs={{0,192},{64,0},{128,64},{192,128},{1,193},{65,1},{129,65},{193,129... | collective-permute-start | bytes 835592 | tf_op jit(solution)/shard_map/ppermute | solution.py:191
  164.2 21.9 %collective-permute-start.18 = (bf16[64,2176]{1,0:T(8,128)(2,1)}, bf16[64,2176]{1,0:T(8,128)(2,1)}, u32[]{:S(2)}, u32[]{:S(2)}) collective-permute-start(bf16[64,2176]{1,0:T(8,128)(2,1)} %get-tuple-element.47), channel_id=1, source_target_pairs={{0,192},{64,0},{128,64},{192,128},{1,193},{65,1},{129,65},{193,129... | collective-permute-start | bytes 835592 | tf_op jit(solution)/shard_map/ppermute | solution.py:191
  164.3 24.0 %collective-permute-start.17 = (bf16[64,2176]{1,0:T(8,128)(2,1)}, bf16[64,2176]{1,0:T(8,128)(2,1)}, u32[]{:S(2)}, u32[]{:S(2)}) collective-permute-start(bf16[64,2176]{1,0:T(8,128)(2,1)} %get-tuple-element.45), channel_id=1, source_target_pairs={{0,192},{64,0},{128,64},{192,128},{1,193},{65,1},{129,65},{193,129... | collective-permute-start | bytes 835592 | tf_op jit(solution)/shard_map/ppermute | solution.py:191
  169.3 19.0 %collective-permute-start.15 = (bf16[64,2176]{1,0:T(8,128)(2,1)}, bf16[64,2176]{1,0:T(8,128)(2,1)}, u32[]{:S(2)}, u32[]{:S(2)}) collective-permute-start(bf16[64,2176]{1,0:T(8,128)(2,1)} %add_convert_fusion.3), channel_id=1, source_target_pairs={{0,64},{64,128},{128,192},{192,0},{1,65},{65,129},{129,193},{193,1... | collective-permute-start | bytes 835592 | tf_op jit(solution)/shard_map/ppermute | solution.py:191
  172.4 31.7 %all-to-all-start.1 = ((bf16[64,2,2176]{2,1,0:T(2,128)(2,1)}), bf16[64,2,2176]{2,1,0:T(2,128)(2,1)}, u32[]{:S(2)}, u32[]{:S(2)}) async-start(bf16[64,2,2176]{2,1,0:T(2,128)(2,1)} %all_to_all.31), calls=%async_computation.1 | async-start | bytes 1114112 | tf_op jit(solution)/shard_map/all_to_all | solution.py:216
  187.2 7.9 %collective-permute-start.19 = (bf16[64,2176]{1,0:T(8,128)(2,1)S(1)}, bf16[64,2176]{1,0:T(8,128)(2,1)S(1)}, u32[]{:S(2)}, u32[]{:S(2)}) collective-permute-start(bf16[64,2176]{1,0:T(8,128)(2,1)S(1)} %add_convert_fusion.2), channel_id=1, source_target_pairs={{0,192},{64,0},{128,64},{192,128},{1,193},{65,1},{129,65},{193,129... | collective-permute-start | bytes 835592 | tf_op jit(solution)/shard_map/ppermute | solution.py:191
  204.1 24.7 %all-to-all-start.3 = ((bf16[64,2,2176]{2,1,0:T(2,128)(2,1)}), bf16[64,2,2176]{2,1,0:T(2,128)(2,1)}, u32[]{:S(2)}, u32[]{:S(2)}) async-start(bf16[64,2,2176]{2,1,0:T(2,128)(2,1)} %all_to_all.37), calls=%async_computation.3 | async-start | bytes 1114112 | tf_op jit(solution)/shard_map/all_to_all | solution.py:216
  (20 other events, 122.2 us)
